TPU v7x, 32 devices: a whole 2x2x4 slice. The times are simulated.
32 devices in a mesh: rev: 8 (over y, x, core), row: 4 (over z).
Axes of the slice: x: 2, y: 2, z: 4, core: 2. Of those that a mesh axis runs over, the one named last changes fastest.
Arguments:
- fields: bfloat16 [8, 16, 1024, 1024], P('rev', None, 'row'), may hold values from -6 to 6
- out_grads: bfloat16 [8, 16, 1024, 1024], P('rev', None, 'row'), may hold values from -6 to 6
- partner: int32 [8], replicated, may hold values from 0 to 7, as said below
- kept_blocks: int32 [8], replicated, may hold values from 1 to 8
- weight_in: float32 [1, 2, 32, 16], replicated, may hold values from -0.75 to 0.75
- bias_in: float32 [1, 2, 16], replicated, may hold values from -3 to 3
- weight_out: float32 [1, 2, 16, 16], replicated, may hold values from -1 to 1
Outputs:
- field_grads: bfloat16 [8, 16, 1024, 1024], P('rev', None, 'row')
- grad_weight_in: float32 [1, 2, 32, 16], replicated
- grad_bias_in: float32 [1, 2, 16], replicated
- grad_weight_out: float32 [1, 2, 16, 16], replicated
- grad_bias_out: float32 [1, 2, 16], replicated
Inputs may be any that keep to these rules, and one draw needn't show every extreme that they name: partner[partner[r]] = r and partner[r] != r for every revision r; some revision r has partner[r] = (r + 4) mod 8.
All inputs are finite; a program needn't handle non-finite values.
Results may differ from a plain program's by a relative error of at most 0.01.
Values may be sent and summed in bfloat16 or wider, within the bound.
A program may use at most 128 MiB of HBM per device.

v0:
```python
import math
import jax
import jax.numpy as jnp
from jax import lax
from jax.sharding import PartitionSpec as P

NH = 1024
NW = 1024
KX = 128
MB = 16
KY = 256
HIGHEST = lax.Precision.HIGHEST


def column_tables(n_cols, n_keep):
    col_index = jnp.arange(n_cols, dtype=jnp.int32)[:, None]
    freq_index = jnp.arange(n_keep, dtype=jnp.int32)[None, :]
    phases = col_index * freq_index % n_cols
    angles = phases.astype(jnp.float32) * (2.0 * math.pi / n_cols)
    return (jnp.cos(angles).astype(jnp.bfloat16), jnp.sin(angles).astype(jnp.bfloat16))


def row_tables(n_rows, n_keep):
    row_index = jnp.arange(n_rows, dtype=jnp.int32)[None, :]
    slot_index = jnp.arange(n_keep, dtype=jnp.int32)
    signed = jnp.where(slot_index < n_keep // 2, slot_index, slot_index - n_keep + n_rows)
    phases = signed[:, None] * row_index % n_rows
    angles = phases.astype(jnp.float32) * (2.0 * math.pi / n_rows)
    return (jnp.cos(angles).astype(jnp.bfloat16), jnp.sin(angles).astype(jnp.bfloat16))


def keep_mask(kept_count, col_index, n_keep):
    slot_index = jnp.arange(n_keep, dtype=jnp.int32)
    row_extent = jnp.where(slot_index < n_keep // 2, slot_index, n_keep - slot_index)
    extent = jnp.maximum(col_index[:, None], row_extent[None, :])
    return (extent < kept_count * MB).astype(jnp.float32)


def complex_layer(weights, biases, real_part, imag_part):

    def mixing(matrix, values):
        return jnp.einsum("bio,bipq->bopq", matrix, values, precision=HIGHEST)

    weight_real = weights[:, 0]
    weight_imag = weights[:, 1]
    out_real = (
        mixing(weight_real, real_part)
        - mixing(weight_imag, imag_part)
        + biases[:, 0, :, None, None]
    )
    out_imag = (
        mixing(weight_imag, real_part)
        + mixing(weight_real, imag_part)
        + biases[:, 1, :, None, None]
    )
    return (out_real, out_imag)


def spectral_mlp(params, own_spec, other_spec):
    weight_in, bias_in, weight_out, bias_out = params
    blocks = weight_in.shape[0]
    block_width = own_spec.shape[1] // blocks
    trailing = own_spec.shape[2:]

    def split_blocks(spectrum):
        return spectrum.reshape((2, blocks, block_width) + trailing)

    joined = jnp.concatenate([split_blocks(own_spec), split_blocks(other_spec)], axis=2)
    hidden_real, hidden_imag = complex_layer(weight_in, bias_in, joined[0], joined[1])
    hidden_real = jax.nn.gelu(hidden_real, approximate=True)
    hidden_imag = jax.nn.gelu(hidden_imag, approximate=True)
    out_real, out_imag = complex_layer(weight_out, bias_out, hidden_real, hidden_imag)
    return jnp.stack([out_real, out_imag]).reshape((2, blocks * block_width) + trailing)


def mlp_backward(params, own_spec, other_spec, cotangent):
    unused, pullback = jax.vjp(spectral_mlp, params, own_spec, other_spec)
    return pullback(cotangent)


def column_pass(field, col_cos, col_sin):
    channels, n_rows, n_cols = field.shape
    flattened = field.reshape(channels * n_rows, n_cols)
    real_cols = jnp.dot(flattened, col_cos, preferred_element_type=jnp.float32)
    imag_cols = -jnp.dot(flattened, col_sin, preferred_element_type=jnp.float32)
    return jnp.stack([real_cols, imag_cols]).astype(jnp.bfloat16).reshape(2, channels, n_rows, -1)


def row_spectrum(column_spec, row_cos, row_sin):
    with_cos = jnp.einsum("schk,jh->sckj", column_spec, row_cos, preferred_element_type=jnp.float32)
    with_sin = jnp.einsum("schk,jh->sckj", column_spec, row_sin, preferred_element_type=jnp.float32)
    real_part = with_cos[0] + with_sin[1]
    imag_part = with_cos[1] - with_sin[0]
    return jnp.stack([real_part, imag_part]) * (1.0 / math.sqrt(NH * NW))


def inverse_rows(total, row_cos, row_sin):
    with_cos = jnp.einsum("sckj,jh->schk", total, row_cos, preferred_element_type=jnp.float32)
    with_sin = jnp.einsum("sckj,jh->schk", total, row_sin, preferred_element_type=jnp.float32)
    real_part = with_cos[0] - with_sin[1]
    imag_part = with_sin[0] + with_cos[1]
    return jnp.stack([real_part, imag_part]).astype(jnp.bfloat16)


def inverse_cols(rows_spec, col_cos, col_sin):
    channels, n_rows, n_keep = rows_spec.shape[1:]
    real_rows = rows_spec[0].reshape(channels * n_rows, n_keep)
    imag_rows = rows_spec[1].reshape(channels * n_rows, n_keep)
    result_real = jnp.einsum("hk,wk->hw", real_rows, col_cos, preferred_element_type=jnp.float32)
    result_imag = jnp.einsum("hk,wk->hw", imag_rows, col_sin, preferred_element_type=jnp.float32)
    field = (result_real - result_imag) * (1.0 / math.sqrt(NH * NW))
    return field.astype(jnp.bfloat16).reshape(channels, n_rows, -1)


def local(fields, out_grads, partner, kept_blocks, weight_in, bias_in, weight_out):
    col_cos, col_sin = column_tables(NW, KX)
    row_cos, row_sin = row_tables(NH, KY)
    own_rev = lax.axis_index("rev")
    row_rank = lax.axis_index("row")
    local_cols = KX // lax.axis_size("row")
    field_cols = column_pass(fields[0], col_cos, col_sin)
    grad_cols = column_pass(out_grads[0], col_cos, col_sin)
    spectra = row_spectrum(
        lax.all_to_all(field_cols, "row", split_axis=3, concat_axis=2, tiled=True), row_cos, row_sin
    )
    grad_spec = row_spectrum(
        lax.all_to_all(grad_cols, "row", split_axis=3, concat_axis=2, tiled=True), row_cos, row_sin
    )

    def route(spectrum):
        target = partner[own_rev]
        slot_array = jnp.zeros((lax.axis_size("rev"),) + spectrum.shape, spectrum.dtype)
        slot_array = lax.dynamic_update_index_in_dim(slot_array, spectrum, target, 0)
        received = lax.all_to_all(slot_array, "rev", split_axis=0, concat_axis=0, tiled=True)
        return lax.dynamic_index_in_dim(received, target, 0, keepdims=False)

    partner_spec = route(spectra.astype(jnp.bfloat16)).astype(jnp.float32)
    col_index = row_rank * local_cols + jnp.arange(local_cols, dtype=jnp.int32)
    keep_local = keep_mask(kept_blocks[own_rev], col_index, KY)
    params = (weight_in, bias_in, weight_out, jnp.zeros_like(bias_in))
    param_grads, own_grads, other_grads = mlp_backward(
        params, spectra, partner_spec, grad_spec * keep_local[None, None]
    )
    returned = route(other_grads.astype(jnp.bfloat16)).astype(jnp.float32)
    total = (own_grads + returned).astype(jnp.bfloat16)
    rows_spec = inverse_rows(total, row_cos, row_sin)
    field_grads = inverse_cols(
        lax.all_to_all(rows_spec, "row", split_axis=2, concat_axis=3, tiled=True), col_cos, col_sin
    )
    summed = lax.psum(
        (param_grads[0], param_grads[1], param_grads[2], param_grads[3]), ("rev", "row")
    )
    grad_scale = 1.0 / math.sqrt(lax.axis_size("rev") * KX * KY)
    return (
        field_grads[None],
        summed[0] * grad_scale,
        summed[1] * grad_scale,
        summed[2] * grad_scale,
        summed[3] * grad_scale,
    )


def solution(mesh):
    placed = (P("rev", None, "row", None), P("rev", None, "row", None), P(), P(), P(), P(), P())
    return jax.shard_map(
        local,
        mesh=mesh,
        in_specs=placed,
        out_specs=(P("rev", None, "row", None), P(), P(), P(), P()),
        check_vma=False,
    )
```

profile of v0, /device:TPU:0, one launch (start us, length us, event | category | flops | bytes accessed | tf_op | source)
XLA Modules:
  0.0 385.1 jit_solution(9175087213200670544)
XLA Ops:
  0.6 8.1 %fusion.1 = bf16[128,4096]{1,0:T(8,128)(2,1)S(1)} fusion(bf16[4096,1024]{1,0:T(8,128)(2,1)} %bitcast.364), kind=kOutput, calls=%fused_computation.4 | convolution fusion | flops 1076756480 | bytes 9437184 | tf_op jit(solution)/shard_map/dot_general | solution.py:85
  8.8 4.6 %convolution_convert_fusion = bf16[128,4096]{1,0:T(8,128)(2,1)S(1)} fusion(bf16[4096,1024]{1,0:T(8,128)(2,1)S(1)} %bitcast.365), kind=kOutput, calls=%fused_computation.5 | convolution fusion | flops 1076232192 | bytes 9437184 | tf_op jit(solution)/shard_map/dot_general | solution.py:84
  13.9 1.5 pad_maximum_fusion.1
  15.4 6.5 %all-to-all-start.1 = ((bf16[2,16,256,128]{2,1,0,3:T(8,128)(2,1)}), bf16[2,16,256,128]{2,1,0,3:T(8,128)(2,1)S(1)}, u32[]{:S(2)}, u32[]{:S(2)}) async-start(bf16[2,16,256,128]{2,1,0,3:T(8,128)(2,1)} %pad_maximum_fusion.1), calls=%async_computation.1 | async-start | bytes 4194304 | tf_op jit(solution)/shard_map/all_to_all | solution.py:124
  21.9 8.0 %fusion = bf16[128,4096]{1,0:T(8,128)(2,1)S(1)} fusion(bf16[4096,1024]{1,0:T(8,128)(2,1)} %bitcast.366), kind=kOutput, calls=%fused_computation.3 | convolution fusion | flops 1076756480 | bytes 9437184 | tf_op jit(solution)/shard_map/dot_general | solution.py:85
  30.2 8.0 %convolution_convert_fusion.1 = bf16[128,4096]{1,0:T(8,128)(2,1)S(1)} fusion(bf16[4096,1024]{1,0:T(8,128)(2,1)} %bitcast.367), kind=kOutput, calls=%fused_computation.6 | convolution fusion | flops 1076232192 | bytes 9437184 | tf_op jit(solution)/shard_map/dot_general | solution.py:84
  38.4 1.6 pad_maximum_fusion
  40.0 30.2 %all-to-all-done.1 = bf16[2,16,256,128]{2,1,0,3:T(8,128)(2,1)S(1)} async-done(((bf16[2,16,256,128]{2,1,0,3:T(8,128)(2,1)}), bf16[2,16,256,128]{2,1,0,3:T(8,128)(2,1)S(1)}, u32[]{:S(2)}, u32[]{:S(2)}) %all-to-all-start.1) | async-done | bytes 2097184 | tf_op jit(solution)/shard_map/all_to_all | solution.py:124
  70.1 1.3 copy-done
  71.4 4.0 %all-to-all-start = ((bf16[2,16,256,128]{2,1,0,3:T(8,128)(2,1)}), bf16[2,16,256,128]{2,1,0,3:T(8,128)(2,1)S(1)}, u32[]{:S(2)}, u32[]{:S(2)}) async-start(bf16[2,16,256,128]{2,1,0,3:T(8,128)(2,1)} %pad_maximum_fusion), calls=%async_computation | async-start | bytes 4194304 | tf_op jit(solution)/shard_map/all_to_all | solution.py:127
  78.0 4.5 %copy.142 = bf16[2,16,256,4,32]{2,3,4,1,0:T(4,128)(2,1)} copy(bf16[2,16,256,4,32]{2,1,0,4,3:T(8,128)(2,1)} %bitcast.346) | data formatting | bytes 4194304 | tf_op jit(solution)/shard_map/all_to_all | solution.py:124
  82.5 4.4 %all_to_all.50 = bf16[2,16,1024,32]{2,3,1,0:T(8,128)(2,1)} reshape(bf16[2,16,4,256,32]{3,2,4,1,0:T(4,128)(2,1)} %bitcast.347) | data formatting | bytes 4194304 | tf_op jit(solution)/shard_map/all_to_all | solution.py:124
  87.0 6.3 %fusion.88 = f32[2,16,32,256]{3,2,1,0:T(8,128)S(1)} fusion(bf16[2,16,1024,32]{2,3,1,0:T(8,128)(2,1)} %all_to_all.50, s32[256]{0:T(256)S(1)} %compare_select_fusion.1), kind=kOutput, calls=%fused_computation.150 | convolution fusion | flops 540803072 | bytes 3146752 | tf_op jit(solution)/shard_map/schk,jh->sckj/dot_general | solution.py:91
  93.2 4.5 %fusion.93 = f32[2,16,32,256]{3,2,1,0:T(8,128)S(1)} fusion(bf16[2,16,1024,32]{2,3,1,0:T(8,128)(2,1)S(1)} %copy-done.4, s32[256]{0:T(256)S(1)} %compare_select_fusion.1), kind=kOutput, calls=%fused_computation.152 | convolution fusion | flops 540803072 | bytes 3146752 | tf_op jit(solution)/shard_map/schk,jh->sckj/dot_general | solution.py:90
  97.9 2.5 broadcast.158.clone
  101.4 21.7 %all-to-all-done = bf16[2,16,256,128]{2,1,0,3:T(8,128)(2,1)S(1)} async-done(((bf16[2,16,256,128]{2,1,0,3:T(8,128)(2,1)}), bf16[2,16,256,128]{2,1,0,3:T(8,128)(2,1)S(1)}, u32[]{:S(2)}, u32[]{:S(2)}) %all-to-all-start) | async-done | bytes 2097184 | tf_op jit(solution)/shard_map/all_to_all | solution.py:127
  123.1 4.6 %all-to-all-start.2 = ((bf16[8,2,16,32,256]{4,3,2,1,0:T(8,128)(2,1)}), bf16[8,2,16,32,256]{4,3,2,1,0:T(8,128)(2,1)}, u32[]{:S(2)}, u32[]{:S(2)}) async-start(bf16[8,2,16,32,256]{4,3,2,1,0:T(8,128)(2,1)} %fusion.62), calls=%async_computation.2 | async-start | bytes 8388608 | tf_op jit(solution)/shard_map/all_to_all | solution.py:134
  129.1 3.0 copy.143
  132.0 3.4 all_to_all.46
  136.5 4.5 %fusion.90 = f32[2,16,32,256]{3,2,1,0:T(8,128)S(1)} fusion(bf16[2,16,1024,32]{2,3,1,0:T(8,128)(2,1)S(1)} %all_to_all.46, s32[256]{0:T(256)S(1)} %compare_select_fusion.1), kind=kOutput, calls=%fused_computation.151 | convolution fusion | flops 540803072 | bytes 3146752 | tf_op jit(solution)/shard_map/schk,jh->sckj/dot_general | solution.py:91
  141.1 4.5 %fusion.95 = f32[2,16,32,256]{3,2,1,0:T(8,128)S(1)} fusion(bf16[2,16,1024,32]{2,3,1,0:T(8,128)(2,1)S(1)} %all_to_all.46, s32[256]{0:T(256)S(1)} %compare_select_fusion.1), kind=kOutput, calls=%fused_computation.153 | convolution fusion | flops 540803072 | bytes 3146752 | tf_op jit(solution)/shard_map/schk,jh->sckj/dot_general | solution.py:90
  147.0 1.7 fusion.106
  148.7 1.7 fusion.108
  150.4 26.4 %all-to-all-done.2 = bf16[8,2,16,32,256]{4,3,2,1,0:T(8,128)(2,1)} async-done(((bf16[8,2,16,32,256]{4,3,2,1,0:T(8,128)(2,1)}), bf16[8,2,16,32,256]{4,3,2,1,0:T(8,128)(2,1)}, u32[]{:S(2)}, u32[]{:S(2)}) %all-to-all-start.2) | async-done | bytes 4194336 | tf_op jit(solution)/shard_map/all_to_all | solution.py:134
  178.7 1.7 fusion.39
  180.4 1.3 fusion.41
  181.7 1.3 fusion.5
  183.0 1.3 fusion.202
  186.4 1.3 fusion.4
  187.7 1.3 fusion.201
  191.0 2.5 fusion.28
  194.1 51.6 %all_to_all.61 = bf16[8,2,16,32,256]{4,3,2,1,0:T(8,128)(2,1)S(1)} all-to-all(bf16[8,2,16,32,256]{4,3,2,1,0:T(8,128)(2,1)S(1)} %fusion.64), channel_id=1, replica_groups=mesh['rev'=8,'row'=4] {'rev'}, dimensions={0} | all-to-all | bytes 8388608 | tf_op jit(solution)/shard_map/all_to_all | solution.py:134
  245.8 4.6 %convolution_bitcast_fusion = f32[2,16,1024,32]{2,3,1,0:T(8,128)S(1)} fusion(bf16[2,16,32,256]{3,2,1,0:T(8,128)(2,1)S(1)} %fusion.22, s32[256]{0:T(256)S(1)} %compare_select_fusion.1), kind=kOutput, calls=%fused_computation.7 | convolution fusion | flops 540803072 | bytes 4719616 | tf_op jit(solution)/shard_map/sckj,jh->schk/dot_general | solution.py:99
  250.4 4.5 %convolution_bitcast_fusion.1 = f32[2,16,1024,32]{2,3,1,0:T(8,128)S(1)} fusion(bf16[2,16,32,256]{3,2,1,0:T(8,128)(2,1)S(1)} %fusion.22, s32[256]{0:T(256)S(1)} %compare_select_fusion.1), kind=kOutput, calls=%fused_computation.8 | convolution fusion | flops 540803072 | bytes 4719616 | tf_op jit(solution)/shard_map/sckj,jh->schk/dot_general | solution.py:98
  254.9 1.2 fusion.3
  256.1 1.5 pad_maximum_fusion.2
  257.6 12.5 %copy.77 = bf16[2,16,1024,32]{3,1,0,2:T(8,128)(2,1)} copy(bf16[2,16,1024,32]{2,3,1,0:T(8,128)(2,1)} %pad_maximum_fusion.2) | data formatting | bytes 4194304 | tf_op jit(solution)/shard_map/stack | solution.py:102
  270.1 10.7 %reshape.381 = bf16[4,2,131072]{2,1,0:T(2,128)(2,1)} reshape(bf16[1024,2,16,32]{3,2,1,0:T(8,128)(2,1)} %bitcast.340) | data formatting | bytes 4194304
  280.8 4.4 %all-to-all-start.4 = ((bf16[4,2,131072]{2,1,0:T(2,128)(2,1)}), bf16[4,2,131072]{2,1,0:T(2,128)(2,1)}, u32[]{:S(2)}, u32[]{:S(2)}) async-start(bf16[4,2,131072]{2,1,0:T(2,128)(2,1)} %reshape.381), calls=%async_computation.4 | async-start | bytes 4194304 | tf_op jit(solution)/shard_map/all_to_all | solution.py:148
  285.3 1.4 convolution_bitcast_fusion.2
  286.7 1.4 convolution_bitcast_fusion.4
  288.1 1.4 fusion.9
  289.5 1.4 fusion.11
  295.2 57.3 %all-reduce.10 = (f32[1,2,32,16]{2,3,1,0:T(8,128)S(1)}, f32[1,2,16]{2,1,0:T(2,128)S(1)}, f32[1,2,16,16]{2,3,1,0:T(8,128)S(1)}, f32[1,2,16]{2,1,0:T(2,128)S(1)}) all-reduce(f32[1,2,32,16]{2,3,1,0:T(8,128)S(1)} %pad_add_fusion.2, f32[1,2,16]{2,1,0:T(2,128)S(1)} %pad_add_fusion.4, ...), channel_id=1, replica_groups=mesh['rev'=8,'row'=4] {'rev','row'}, use_global_device_ids=true, to_apply=%region_0.1 | all-reduce | flops 1600 | bytes 12800 | tf_op jit(solution)/shard_map/psum | solution.py:150
  354.4 7.3 %reshape.382 = bf16[1024,2,16,32]{3,2,1,0:T(8,128)(2,1)} reshape(bf16[4,2,131072]{2,1,0:T(2,128)(2,1)} %all-to-all-done.4) | data formatting | bytes 4194304
  361.8 10.9 %copy.78 = bf16[2,16,4,256,32]{3,1,4,2,0:T(8,128)(2,1)S(1)} copy(bf16[2,16,4,256,32]{4,1,0,3,2:T(8,128)(2,1)} %bitcast.341) | data formatting | bytes 4194304 | tf_op jit(solution)/shard_map/all_to_all | solution.py:148
  373.8 4.4 %fusion.110 = f32[4096,1024]{1,0:T(8,128)S(1)} fusion(bf16[4096,128]{0,1:T(8,128)(2,1)S(1)} %bitcast.349), kind=kOutput, calls=%fused_computation.171 | convolution fusion | flops 1075707904 | bytes 17825792 | tf_op jit(solution)/shard_map/hk,wk->hw/dot_general | solution.py:109
  378.2 6.5 %multiply_convert_fusion = bf16[4096,1024]{1,0:T(8,128)(2,1)} fusion(f32[4096,1024]{1,0:T(8,128)S(1)} %fusion.110, bf16[4096,128]{0,1:T(8,128)(2,1)S(1)} %bitcast.343), kind=kOutput, calls=%fused_computation | convolution fusion | flops 1088290816 | bytes 26214400 | tf_op jit(solution)/shard_map/hk,wk->hw/dot_general | solution.py:110
  (83 shorter events, 19.9 us)
Async XLA Ops:
  0.6 8.1 %copy-start.18 = (bf16[1,16,256,1024]{3,2,1,0:T(8,128)(2,1)S(1)}, bf16[1,16,256,1024]{3,2,1,0:T(8,128)(2,1)}, u32[]{:S(2)}) copy-start(bf16[1,16,256,1024]{3,2,1,0:T(8,128)(2,1)} %param.7) | copy-start | bytes 25165828
  15.4 54.7 %all-to-all-start.1 = ((bf16[2,16,256,128]{2,1,0,3:T(8,128)(2,1)}), bf16[2,16,256,128]{2,1,0,3:T(8,128)(2,1)S(1)}, u32[]{:S(2)}, u32[]{:S(2)}) async-start(bf16[2,16,256,128]{2,1,0,3:T(8,128)(2,1)} %pad_maximum_fusion.1), calls=%async_computation.1 | async-start | bytes 4194304 | tf_op jit(solution)/shard_map/all_to_all | solution.py:124
  40.0 35.5 %copy-start.19 = (s32[8]{0:T(128)S(1)}, s32[8]{0:T(128)}, u32[]{:S(2)}) copy-start(s32[8]{0:T(128)} %param.9) | copy-start | bytes 100
  70.1 1.3 copy-start
  71.4 51.7 %all-to-all-start = ((bf16[2,16,256,128]{2,1,0,3:T(8,128)(2,1)}), bf16[2,16,256,128]{2,1,0,3:T(8,128)(2,1)S(1)}, u32[]{:S(2)}, u32[]{:S(2)}) async-start(bf16[2,16,256,128]{2,1,0,3:T(8,128)(2,1)} %pad_maximum_fusion), calls=%async_computation | async-start | bytes 4194304 | tf_op jit(solution)/shard_map/all_to_all | solution.py:127
  87.0 6.3 %copy-start.4 = (bf16[2,16,1024,32]{2,3,1,0:T(8,128)(2,1)S(1)}, bf16[2,16,1024,32]{2,3,1,0:T(8,128)(2,1)}, u32[]{:S(2)}) copy-start(bf16[2,16,1024,32]{2,3,1,0:T(8,128)(2,1)} %all_to_all.50) | copy-start | bytes 6291460
  101.4 26.3 %copy-start.20 = (s32[8]{0:T(128)S(1)}, s32[8]{0:T(128)}, u32[]{:S(2)}) copy-start(s32[8]{0:T(128)} %param.10) | copy-start | bytes 100
  101.4 27.5 %copy-start.17 = (f32[1,2,16]{2,1,0:T(2,128)S(1)}, f32[1,2,16]{2,1,0:T(2,128)}, u32[]{:S(2)}) copy-start(f32[1,2,16]{2,1,0:T(2,128)} %param.12) | copy-start | bytes 388
  123.1 53.7 %all-to-all-start.2 = ((bf16[8,2,16,32,256]{4,3,2,1,0:T(8,128)(2,1)}), bf16[8,2,16,32,256]{4,3,2,1,0:T(8,128)(2,1)}, u32[]{:S(2)}, u32[]{:S(2)}) async-start(bf16[8,2,16,32,256]{4,3,2,1,0:T(8,128)(2,1)} %fusion.62), calls=%async_computation.2 | async-start | bytes 8388608 | tf_op jit(solution)/shard_map/all_to_all | solution.py:134
  145.8 1.2 copy-start.16
  147.0 1.7 copy-start.1
  147.0 30.9 %copy-start.3 = (f32[2,1,16,32,256]{4,3,2,1,0:T(8,128)S(1)}, f32[2,1,16,32,256]{4,3,2,1,0:T(8,128)}, u32[]{:S(2)}) copy-start(f32[2,1,16,32,256]{4,3,2,1,0:T(8,128)} %maximum_multiply_fusion.1) | copy-start | bytes 3145732
  178.0 0.7 copy-start.15
  180.4 2.6 copy-start.5
  180.4 2.6 copy-start.14
  183.0 2.3 copy-start.9
  185.3 2.3 copy-start.7
  185.3 2.3 copy-start.13
  187.6 2.3 copy-start.11
  280.8 73.6 %all-to-all-start.4 = ((bf16[4,2,131072]{2,1,0:T(2,128)(2,1)}), bf16[4,2,131072]{2,1,0:T(2,128)(2,1)}, u32[]{:S(2)}, u32[]{:S(2)}) async-start(bf16[4,2,131072]{2,1,0:T(2,128)(2,1)} %reshape.381), calls=%async_computation.4 | async-start | bytes 4194304 | tf_op jit(solution)/shard_map/all_to_all | solution.py:148
  286.7 4.3 %copy-start.8 = (f32[16,32,256]{2,1,0:T(8,128)S(1)}, f32[16,32,256]{2,1,0:T(8,128)}, u32[]{:S(2)}) copy-start(f32[16,32,256]{2,1,0:T(8,128)} %get-tuple-element.36) | copy-start | bytes 1572868
  286.7 4.3 %copy-start.12 = (f32[32,256,16]{1,2,0:T(8,128)S(1)}, f32[32,256,16]{1,2,0:T(8,128)}, u32[]{:S(2)}) copy-start(f32[32,256,16]{1,2,0:T(8,128)} %copy-done.11) | copy-start | bytes 1572868
  288.1 3.9 %copy-start.6 = (f32[16,32,256]{2,1,0:T(8,128)S(1)}, f32[16,32,256]{2,1,0:T(8,128)}, u32[]{:S(2)}) copy-start(f32[16,32,256]{2,1,0:T(8,128)} %get-tuple-element.37) | copy-start | bytes 1572868
  288.1 3.9 %copy-start.10 = (f32[32,256,16]{1,2,0:T(8,128)S(1)}, f32[32,256,16]{1,2,0:T(8,128)}, u32[]{:S(2)}) copy-start(f32[32,256,16]{1,2,0:T(8,128)} %copy-done.9) | copy-start | bytes 1572868
  289.5 3.5 copy-start.2
where the time goes:
time: 393 us; the launch traced here: 385 us
  blocking collectives  109 us (28%)
  matrix products  93.7 us (24%)
  waiting for transfers between devices  78.3 us (20%)
  local copies, waits for them, and re-layouts  65.6 us (17%)
  starting transfers between devices  19.5 us (5%)
  other arithmetic  14.8 us (4%)
  between operations  4.32 us (1%)
    psum x1, blocking collectives, local(): lax.psum((param_grads[0], param_grads[1], param_grads[2], param_grads[3])...  57.3 us
    all_to_all x1, blocking collectives, route(): lax.all_to_all(slot_array, 'rev', split_axis=0, concat_axis=0, tiled=True)  51.6 us
    all_to_all x1, waiting for transfers between devices, local(): lax.all_to_all(field_cols, 'row', split_axis=3, concat_axis=2, tiled=True)  30.2 us
    all_to_all x1, waiting for transfers between devices, route(): lax.all_to_all(slot_array, 'rev', split_axis=0, concat_axis=0, tiled=True)  26.4 us
    dot_general x20, matrix products, mixing(): return jnp.einsum('bio,bipq->bopq', matrix, values, precision=HIGHEST)  25.2 us
    unnamed x51, local copies, waits for them, and re-layouts  22.5 us
    all_to_all x1, waiting for transfers between devices, local(): lax.all_to_all(grad_cols, 'row', split_axis=3, concat_axis=2, tiled=True)  21.7 us
    dot_general x2, matrix products, column_pass(): imag_cols = -jnp.dot(flattened, col_sin, preferred_element_type=jnp.float32)  16.1 us
  transfers between devices with their start and end apart: 4, of which 3 were waited for; matrix products, arithmetic and copies ran while one was open for 18% of the time, Pallas kernels for 0%

commit v1 on v0

--- a/solution.py
+++ b/solution.py
@@ -147,9 +147,9 @@
     field_grads = inverse_cols(
         lax.all_to_all(rows_spec, "row", split_axis=2, concat_axis=3, tiled=True), col_cos, col_sin
     )
-    summed = lax.psum(
-        (param_grads[0], param_grads[1], param_grads[2], param_grads[3]), ("rev", "row")
-    )
+    summed = (param_grads[0], param_grads[1], param_grads[2], param_grads[3])
+    for mesh_axis in ("row", "rev"):
+        summed = lax.psum(summed, mesh_axis)
     grad_scale = 1.0 / math.sqrt(lax.axis_size("rev") * KX * KY)
     return (
         field_grads[None],

time: 393 us -> 406 us (1.033)
  blocking collectives: 109 us -> 122 us
    psum x1 -> x2, blocking collectives: 57.3 us -> 70 us  [local(): summed = lax.psum(summed, mesh_axis)]
  transfers between devices with their start and end apart: 4 -> 4, of which waited for: 3 -> 3; matrix products, arithmetic and copies ran while one was open for 18% -> 17% of each run, Pallas kernels for 0% -> 0%
where the time goes in v1:
time: 406 us; the launch traced here: 398 us
  blocking collectives  122 us (30%)
  matrix products  93.6 us (23%)
  waiting for transfers between devices  78.3 us (19%)
  local copies, waits for them, and re-layouts  65.6 us (16%)
  starting transfers between devices  19.6 us (5%)
  other arithmetic  15.3 us (4%)
  between operations  4.31 us (1%)
    psum x2, blocking collectives, local(): summed = lax.psum(summed, mesh_axis)  70 us
    all_to_all x1, blocking collectives, route(): lax.all_to_all(slot_array, 'rev', split_axis=0, concat_axis=0, tiled=True)  51.6 us
    all_to_all x1, waiting for transfers between devices, local(): lax.all_to_all(field_cols, 'row', split_axis=3, concat_axis=2, tiled=True)  30.1 us
    all_to_all x1, waiting for transfers between devices, route(): lax.all_to_all(slot_array, 'rev', split_axis=0, concat_axis=0, tiled=True)  26.5 us
    dot_general x20, matrix products, mixing(): return jnp.einsum('bio,bipq->bopq', matrix, values, precision=HIGHEST)  25.2 us
    unnamed x51, local copies, waits for them, and re-layouts  22.5 us
    all_to_all x1, waiting for transfers between devices, local(): lax.all_to_all(grad_cols, 'row', split_axis=3, concat_axis=2, tiled=True)  21.7 us
    dot_general x2, matrix products, column_pass(): imag_cols = -jnp.dot(flattened, col_sin, preferred_element_type=jnp.float32)  16.1 us
  transfers between devices with their start and end apart: 4, of which 3 were waited for; matrix products, arithmetic and copies ran while one was open for 17% of the time, Pallas kernels for 0%

profile of v1, /device:TPU:0, one launch (start us, length us, event | category | flops | bytes accessed | tf_op | source)
XLA Modules:
  0.0 398.4 jit_solution(2357647858148265642)
XLA Ops:
  0.6 8.1 %fusion.1 = bf16[128,4096]{1,0:T(8,128)(2,1)S(1)} fusion(bf16[4096,1024]{1,0:T(8,128)(2,1)} %bitcast.364), kind=kOutput, calls=%fused_computation.4 | convolution fusion | flops 1076756480 | bytes 9437184 | tf_op jit(solution)/shard_map/dot_general | solution.py:85
  8.8 4.6 %convolution_convert_fusion = bf16[128,4096]{1,0:T(8,128)(2,1)S(1)} fusion(bf16[4096,1024]{1,0:T(8,128)(2,1)S(1)} %bitcast.365), kind=kOutput, calls=%fused_computation.5 | convolution fusion | flops 1076232192 | bytes 9437184 | tf_op jit(solution)/shard_map/dot_general | solution.py:84
  13.9 1.5 pad_maximum_fusion.1
  15.4 6.5 %all-to-all-start.1 = ((bf16[2,16,256,128]{2,1,0,3:T(8,128)(2,1)}), bf16[2,16,256,128]{2,1,0,3:T(8,128)(2,1)S(1)}, u32[]{:S(2)}, u32[]{:S(2)}) async-start(bf16[2,16,256,128]{2,1,0,3:T(8,128)(2,1)} %pad_maximum_fusion.1), calls=%async_computation.1 | async-start | bytes 4194304 | tf_op jit(solution)/shard_map/all_to_all | solution.py:124
  21.9 8.0 %fusion = bf16[128,4096]{1,0:T(8,128)(2,1)S(1)} fusion(bf16[4096,1024]{1,0:T(8,128)(2,1)} %bitcast.366), kind=kOutput, calls=%fused_computation.3 | convolution fusion | flops 1076756480 | bytes 9437184 | tf_op jit(solution)/shard_map/dot_general | solution.py:85
  30.2 8.0 %convolution_convert_fusion.1 = bf16[128,4096]{1,0:T(8,128)(2,1)S(1)} fusion(bf16[4096,1024]{1,0:T(8,128)(2,1)} %bitcast.367), kind=kOutput, calls=%fused_computation.6 | convolution fusion | flops 1076232192 | bytes 9437184 | tf_op jit(solution)/shard_map/dot_general | solution.py:84
  38.4 1.6 pad_maximum_fusion
  40.0 30.1 %all-to-all-done.1 = bf16[2,16,256,128]{2,1,0,3:T(8,128)(2,1)S(1)} async-done(((bf16[2,16,256,128]{2,1,0,3:T(8,128)(2,1)}), bf16[2,16,256,128]{2,1,0,3:T(8,128)(2,1)S(1)}, u32[]{:S(2)}, u32[]{:S(2)}) %all-to-all-start.1) | async-done | bytes 2097184 | tf_op jit(solution)/shard_map/all_to_all | solution.py:124
  70.1 1.3 copy-done
  71.4 4.0 %all-to-all-start = ((bf16[2,16,256,128]{2,1,0,3:T(8,128)(2,1)}), bf16[2,16,256,128]{2,1,0,3:T(8,128)(2,1)S(1)}, u32[]{:S(2)}, u32[]{:S(2)}) async-start(bf16[2,16,256,128]{2,1,0,3:T(8,128)(2,1)} %pad_maximum_fusion), calls=%async_computation | async-start | bytes 4194304 | tf_op jit(solution)/shard_map/all_to_all | solution.py:127
  78.0 4.5 %copy.142 = bf16[2,16,256,4,32]{2,3,4,1,0:T(4,128)(2,1)} copy(bf16[2,16,256,4,32]{2,1,0,4,3:T(8,128)(2,1)} %bitcast.346) | data formatting | bytes 4194304 | tf_op jit(solution)/shard_map/all_to_all | solution.py:124
  82.5 4.4 %all_to_all.50 = bf16[2,16,1024,32]{2,3,1,0:T(8,128)(2,1)} reshape(bf16[2,16,4,256,32]{3,2,4,1,0:T(4,128)(2,1)} %bitcast.347) | data formatting | bytes 4194304 | tf_op jit(solution)/shard_map/all_to_all | solution.py:124
  87.0 6.3 %fusion.88 = f32[2,16,32,256]{3,2,1,0:T(8,128)S(1)} fusion(bf16[2,16,1024,32]{2,3,1,0:T(8,128)(2,1)} %all_to_all.50, s32[256]{0:T(256)S(1)} %compare_select_fusion.1), kind=kOutput, calls=%fused_computation.150 | convolution fusion | flops 540803072 | bytes 3146752 | tf_op jit(solution)/shard_map/schk,jh->sckj/dot_general | solution.py:91
  93.3 4.5 %fusion.93 = f32[2,16,32,256]{3,2,1,0:T(8,128)S(1)} fusion(bf16[2,16,1024,32]{2,3,1,0:T(8,128)(2,1)S(1)} %copy-done.4, s32[256]{0:T(256)S(1)} %compare_select_fusion.1), kind=kOutput, calls=%fused_computation.152 | convolution fusion | flops 540803072 | bytes 3146752 | tf_op jit(solution)/shard_map/schk,jh->sckj/dot_general | solution.py:90
  98.0 2.5 broadcast.158.clone
  101.4 21.7 %all-to-all-done = bf16[2,16,256,128]{2,1,0,3:T(8,128)(2,1)S(1)} async-done(((bf16[2,16,256,128]{2,1,0,3:T(8,128)(2,1)}), bf16[2,16,256,128]{2,1,0,3:T(8,128)(2,1)S(1)}, u32[]{:S(2)}, u32[]{:S(2)}) %all-to-all-start) | async-done | bytes 2097184 | tf_op jit(solution)/shard_map/all_to_all | solution.py:127
  123.1 4.6 %all-to-all-start.2 = ((bf16[8,2,16,32,256]{4,3,2,1,0:T(8,128)(2,1)}), bf16[8,2,16,32,256]{4,3,2,1,0:T(8,128)(2,1)}, u32[]{:S(2)}, u32[]{:S(2)}) async-start(bf16[8,2,16,32,256]{4,3,2,1,0:T(8,128)(2,1)} %fusion.62), calls=%async_computation.2 | async-start | bytes 8388608 | tf_op jit(solution)/shard_map/all_to_all | solution.py:134
  129.1 3.0 copy.143
  132.0 3.4 all_to_all.46
  136.5 4.5 %fusion.90 = f32[2,16,32,256]{3,2,1,0:T(8,128)S(1)} fusion(bf16[2,16,1024,32]{2,3,1,0:T(8,128)(2,1)S(1)} %all_to_all.46, s32[256]{0:T(256)S(1)} %compare_select_fusion.1), kind=kOutput, calls=%fused_computation.151 | convolution fusion | flops 540803072 | bytes 3146752 | tf_op jit(solution)/shard_map/schk,jh->sckj/dot_general | solution.py:91
  141.1 4.5 %fusion.95 = f32[2,16,32,256]{3,2,1,0:T(8,128)S(1)} fusion(bf16[2,16,1024,32]{2,3,1,0:T(8,128)(2,1)S(1)} %all_to_all.46, s32[256]{0:T(256)S(1)} %compare_select_fusion.1), kind=kOutput, calls=%fused_computation.153 | convolution fusion | flops 540803072 | bytes 3146752 | tf_op jit(solution)/shard_map/schk,jh->sckj/dot_general | solution.py:90
  147.0 1.7 fusion.106
  148.7 1.7 fusion.108
  150.3 26.5 %all-to-all-done.2 = bf16[8,2,16,32,256]{4,3,2,1,0:T(8,128)(2,1)} async-done(((bf16[8,2,16,32,256]{4,3,2,1,0:T(8,128)(2,1)}), bf16[8,2,16,32,256]{4,3,2,1,0:T(8,128)(2,1)}, u32[]{:S(2)}, u32[]{:S(2)}) %all-to-all-start.2) | async-done | bytes 4194336 | tf_op jit(solution)/shard_map/all_to_all | solution.py:134
  178.7 1.7 fusion.39
  180.4 1.3 fusion.41
  181.7 1.3 fusion.5
  183.0 1.3 fusion.202
  186.4 1.3 fusion.4
  187.7 1.3 fusion.201
  191.0 2.5 fusion.28
  194.1 51.6 %all_to_all.61 = bf16[8,2,16,32,256]{4,3,2,1,0:T(8,128)(2,1)S(1)} all-to-all(bf16[8,2,16,32,256]{4,3,2,1,0:T(8,128)(2,1)S(1)} %fusion.64), channel_id=1, replica_groups=mesh['rev'=8,'row'=4] {'rev'}, dimensions={0} | all-to-all | bytes 8388608 | tf_op jit(solution)/shard_map/all_to_all | solution.py:134
  245.8 4.6 %convolution_bitcast_fusion = f32[2,16,1024,32]{2,3,1,0:T(8,128)S(1)} fusion(bf16[2,16,32,256]{3,2,1,0:T(8,128)(2,1)S(1)} %fusion.22, s32[256]{0:T(256)S(1)} %compare_select_fusion.1), kind=kOutput, calls=%fused_computation.7 | convolution fusion | flops 540803072 | bytes 4719616 | tf_op jit(solution)/shard_map/sckj,jh->schk/dot_general | solution.py:99
  250.4 4.5 %convolution_bitcast_fusion.1 = f32[2,16,1024,32]{2,3,1,0:T(8,128)S(1)} fusion(bf16[2,16,32,256]{3,2,1,0:T(8,128)(2,1)S(1)} %fusion.22, s32[256]{0:T(256)S(1)} %compare_select_fusion.1), kind=kOutput, calls=%fused_computation.8 | convolution fusion | flops 540803072 | bytes 4719616 | tf_op jit(solution)/shard_map/sckj,jh->schk/dot_general | solution.py:98
  256.1 1.5 pad_maximum_fusion.2
  257.7 12.5 %copy.77 = bf16[2,16,1024,32]{3,1,0,2:T(8,128)(2,1)} copy(bf16[2,16,1024,32]{2,3,1,0:T(8,128)(2,1)} %pad_maximum_fusion.2) | data formatting | bytes 4194304 | tf_op jit(solution)/shard_map/stack | solution.py:102
  270.1 10.7 %reshape.381 = bf16[4,2,131072]{2,1,0:T(2,128)(2,1)} reshape(bf16[1024,2,16,32]{3,2,1,0:T(8,128)(2,1)} %bitcast.340) | data formatting | bytes 4194304
  280.9 4.5 %all-to-all-start.4 = ((bf16[4,2,131072]{2,1,0:T(2,128)(2,1)}), bf16[4,2,131072]{2,1,0:T(2,128)(2,1)}, u32[]{:S(2)}, u32[]{:S(2)}) async-start(bf16[4,2,131072]{2,1,0:T(2,128)(2,1)} %reshape.381), calls=%async_computation.4 | async-start | bytes 4194304 | tf_op jit(solution)/shard_map/all_to_all | solution.py:148
  285.3 1.4 convolution_bitcast_fusion.2
  286.7 1.4 convolution_bitcast_fusion.4
  288.1 1.4 fusion.9
  289.5 1.4 fusion.11
  295.3 47.1 %all-reduce.11 = (f32[1,2,32,16]{2,3,1,0:T(8,128)S(1)}, f32[1,2,16]{2,1,0:T(2,128)S(1)}, f32[1,2,16,16]{2,3,1,0:T(8,128)S(1)}, f32[1,2,16]{2,1,0:T(2,128)S(1)}) all-reduce(f32[1,2,32,16]{2,3,1,0:T(8,128)S(1)} %pad_add_fusion.2, f32[1,2,16]{2,1,0:T(2,128)S(1)} %get-tuple-element.52, ...), channel_id=1, replica_groups=mesh['rev'=8,'row'=4] {'row'}, use_global_device_ids=true, to_apply=%region_0.1 | all-reduce | flops 1600 | bytes 12800 | tf_op jit(solution)/shard_map/psum | solution.py:152
  342.4 22.9 %all-reduce.10 = (f32[1,2,32,16]{2,3,1,0:T(8,128)S(1)}, f32[1,2,16]{2,1,0:T(2,128)S(1)}, f32[1,2,16,16]{2,3,1,0:T(8,128)S(1)}, f32[1,2,16]{2,1,0:T(2,128)S(1)}) all-reduce(f32[1,2,32,16]{2,3,1,0:T(8,128)S(1)} %get-tuple-element.26, f32[1,2,16]{2,1,0:T(2,128)S(1)} %get-tuple-element.27, ...), channel_id=1, replica_groups=mesh['rev'=8,'row'=4] {'rev'}, use_global_device_ids=true, to_apply=%region_1.2 | all-reduce | flops 1600 | bytes 12800 | tf_op jit(solution)/shard_map/psum | solution.py:152
  367.7 7.3 %reshape.382 = bf16[1024,2,16,32]{3,2,1,0:T(8,128)(2,1)} reshape(bf16[4,2,131072]{2,1,0:T(2,128)(2,1)} %all-to-all-done.4) | data formatting | bytes 4194304
  375.1 10.9 %copy.78 = bf16[2,16,4,256,32]{3,1,4,2,0:T(8,128)(2,1)S(1)} copy(bf16[2,16,4,256,32]{4,1,0,3,2:T(8,128)(2,1)} %bitcast.341) | data formatting | bytes 4194304 | tf_op jit(solution)/shard_map/all_to_all | solution.py:148
  387.1 4.4 %fusion.110 = f32[4096,1024]{1,0:T(8,128)S(1)} fusion(bf16[4096,128]{0,1:T(8,128)(2,1)S(1)} %bitcast.349), kind=kOutput, calls=%fused_computation.171 | convolution fusion | flops 1075707904 | bytes 17825792 | tf_op jit(solution)/shard_map/hk,wk->hw/dot_general | solution.py:109
  391.5 6.5 %multiply_convert_fusion = bf16[4096,1024]{1,0:T(8,128)(2,1)} fusion(f32[4096,1024]{1,0:T(8,128)S(1)} %fusion.110, bf16[4096,128]{0,1:T(8,128)(2,1)S(1)} %bitcast.343), kind=kOutput, calls=%fused_computation | convolution fusion | flops 1088290816 | bytes 26214400 | tf_op jit(solution)/shard_map/hk,wk->hw/dot_general | solution.py:110
  (84 shorter events, 21.6 us)
Async XLA Ops:
  0.6 8.1 %copy-start.18 = (bf16[1,16,256,1024]{3,2,1,0:T(8,128)(2,1)S(1)}, bf16[1,16,256,1024]{3,2,1,0:T(8,128)(2,1)}, u32[]{:S(2)}) copy-start(bf16[1,16,256,1024]{3,2,1,0:T(8,128)(2,1)} %param.7) | copy-start | bytes 25165828
  15.4 54.7 %all-to-all-start.1 = ((bf16[2,16,256,128]{2,1,0,3:T(8,128)(2,1)}), bf16[2,16,256,128]{2,1,0,3:T(8,128)(2,1)S(1)}, u32[]{:S(2)}, u32[]{:S(2)}) async-start(bf16[2,16,256,128]{2,1,0,3:T(8,128)(2,1)} %pad_maximum_fusion.1), calls=%async_computation.1 | async-start | bytes 4194304 | tf_op jit(solution)/shard_map/all_to_all | solution.py:124
  40.0 35.5 %copy-start.19 = (s32[8]{0:T(128)S(1)}, s32[8]{0:T(128)}, u32[]{:S(2)}) copy-start(s32[8]{0:T(128)} %param.9) | copy-start | bytes 100
  70.1 1.3 copy-start
  71.4 51.7 %all-to-all-start = ((bf16[2,16,256,128]{2,1,0,3:T(8,128)(2,1)}), bf16[2,16,256,128]{2,1,0,3:T(8,128)(2,1)S(1)}, u32[]{:S(2)}, u32[]{:S(2)}) async-start(bf16[2,16,256,128]{2,1,0,3:T(8,128)(2,1)} %pad_maximum_fusion), calls=%async_computation | async-start | bytes 4194304 | tf_op jit(solution)/shard_map/all_to_all | solution.py:127
  87.0 6.3 %copy-start.4 = (bf16[2,16,1024,32]{2,3,1,0:T(8,128)(2,1)S(1)}, bf16[2,16,1024,32]{2,3,1,0:T(8,128)(2,1)}, u32[]{:S(2)}) copy-start(bf16[2,16,1024,32]{2,3,1,0:T(8,128)(2,1)} %all_to_all.50) | copy-start | bytes 6291460
  101.4 26.3 %copy-start.20 = (s32[8]{0:T(128)S(1)}, s32[8]{0:T(128)}, u32[]{:S(2)}) copy-start(s32[8]{0:T(128)} %param.10) | copy-start | bytes 100
  101.4 27.5 %copy-start.17 = (f32[1,2,16]{2,1,0:T(2,128)S(1)}, f32[1,2,16]{2,1,0:T(2,128)}, u32[]{:S(2)}) copy-start(f32[1,2,16]{2,1,0:T(2,128)} %param.12) | copy-start | bytes 388
  123.1 53.7 %all-to-all-start.2 = ((bf16[8,2,16,32,256]{4,3,2,1,0:T(8,128)(2,1)}), bf16[8,2,16,32,256]{4,3,2,1,0:T(8,128)(2,1)}, u32[]{:S(2)}, u32[]{:S(2)}) async-start(bf16[8,2,16,32,256]{4,3,2,1,0:T(8,128)(2,1)} %fusion.62), calls=%async_computation.2 | async-start | bytes 8388608 | tf_op jit(solution)/shard_map/all_to_all | solution.py:134
  145.8 1.2 copy-start.16
  147.0 1.7 copy-start.1
  147.0 31.0 %copy-start.3 = (f32[2,1,16,32,256]{4,3,2,1,0:T(8,128)S(1)}, f32[2,1,16,32,256]{4,3,2,1,0:T(8,128)}, u32[]{:S(2)}) copy-start(f32[2,1,16,32,256]{4,3,2,1,0:T(8,128)} %maximum_multiply_fusion.1) | copy-start | bytes 3145732
  178.0 0.7 copy-start.15
  180.4 2.6 copy-start.5
  180.4 2.6 copy-start.14
  183.0 2.3 copy-start.9
  185.3 2.3 copy-start.7
  185.3 2.3 copy-start.13
  187.6 2.3 copy-start.11
  280.9 86.9 %all-to-all-start.4 = ((bf16[4,2,131072]{2,1,0:T(2,128)(2,1)}), bf16[4,2,131072]{2,1,0:T(2,128)(2,1)}, u32[]{:S(2)}, u32[]{:S(2)}) async-start(bf16[4,2,131072]{2,1,0:T(2,128)(2,1)} %reshape.381), calls=%async_computation.4 | async-start | bytes 4194304 | tf_op jit(solution)/shard_map/all_to_all | solution.py:148
  286.7 4.3 %copy-start.8 = (f32[16,32,256]{2,1,0:T(8,128)S(1)}, f32[16,32,256]{2,1,0:T(8,128)}, u32[]{:S(2)}) copy-start(f32[16,32,256]{2,1,0:T(8,128)} %get-tuple-element.40) | copy-start | bytes 1572868
  286.7 4.3 %copy-start.12 = (f32[32,256,16]{1,2,0:T(8,128)S(1)}, f32[32,256,16]{1,2,0:T(8,128)}, u32[]{:S(2)}) copy-start(f32[32,256,16]{1,2,0:T(8,128)} %copy-done.11) | copy-start | bytes 1572868
  288.1 3.9 copy-start.6
  288.1 3.9 copy-start.10
  289.5 3.5 copy-start.2
